TPU v7x, 256 devices: a whole 4x4x8 slice. The times are simulated.
256 devices in a mesh: group: 16 (over z, core), dev: 16 (over y, x).
Axes of the slice: x: 4, y: 4, z: 8, core: 2. Of those that a mesh axis runs over, the one named last changes fastest.
Arguments:
- tokens: bfloat16 [1024, 7168], P(('group', 'dev')), may hold values from -6 to 6
- group_ids: int32 [1024, 4], P(('group', 'dev')), may hold values from 0 to 15, as said below
- expert_ids: int32 [1024, 8], P(('group', 'dev')), may hold values from 0 to 63, as said below
- gate_scores: bfloat16 [1024, 8], P(('group', 'dev')), may hold values from 0.099609375 to 1
- w_gate: bfloat16 [7168, 65536], P(None, ('group', 'dev')), may hold values from -0.0625 to 0.0625
- w_up: bfloat16 [7168, 65536], P(None, ('group', 'dev')), may hold values from -0.0625 to 0.0625
- w_down: bfloat16 [65536, 7168], P(('group', 'dev')), may hold values from -0.1875 to 0.1875
Outputs:
- combined: bfloat16 [1024, 7168], P(('group', 'dev'))
Inputs may be any that keep to these rules, and one draw needn't show every extreme that they name: `group_ids`: each row names 4 different groups; among the 4 rows of one aligned block, at most 2 rows name any one group. `expert_ids`: each row names 8 different experts, exactly two in each group of the row's group_ids (expert x lies in group x // 4).
All inputs are finite; a program needn't handle non-finite values.
Results may differ from a plain program's by a relative error of at most 0.014.
Values may be sent and summed in bfloat16 or wider, within the bound.
No kernel may reach another device: no remote copies, remote signals or barrier semaphores. Data moves between devices by JAX's collectives and lax.ppermute only.
A program may use at most 64 MiB of HBM per device.

v0:
```python
import jax
import jax.numpy as jnp
from jax import lax
from jax.sharding import PartitionSpec as P

FF = 1024
EXP_GROUP = 4
CAP = 2


def local(tokens, group_ids, expert_ids, gate_scores, w_gate, w_up, w_down):
    group_count = lax.axis_size("group")
    dev_count = lax.axis_size("dev")
    model_width = tokens.shape[1]
    block_cols = w_gate.shape[1]
    expert_total = group_count * EXP_GROUP
    group_iota = jnp.arange(group_count, dtype=jnp.int32)
    member = jnp.sum((group_ids[:, :, None] == group_iota[None, None, :]).astype(jnp.int32), axis=1)
    before = jnp.cumsum(member, axis=0) - member
    slot_iota = jnp.arange(CAP, dtype=jnp.int32)
    select = (member.T[:, None, :] == 1) & (before.T[:, None, :] == slot_iota[None, :, None])
    select_rows = select.astype(jnp.bfloat16)
    matches = (
        expert_ids[:, :, None] == jnp.arange(expert_total, dtype=jnp.int32)[None, None, :]
    ).astype(jnp.float32)
    coef = jnp.sum(gate_scores.astype(jnp.float32)[:, :, None] * matches, axis=1)
    coef = coef.reshape(-1, group_count, EXP_GROUP).astype(jnp.bfloat16)
    send_rows = jnp.einsum(
        "gst,td->gsd", select_rows, tokens, preferred_element_type=jnp.float32
    ).astype(jnp.bfloat16)
    send_coef = jnp.einsum(
        "gst,tge->gse", select_rows, coef, preferred_element_type=jnp.float32
    ).astype(jnp.bfloat16)
    recv_rows, recv_coef = (
        lax.all_to_all(send_rows, "group", split_axis=0, concat_axis=0, tiled=True),
        lax.all_to_all(send_coef, "group", split_axis=0, concat_axis=0, tiled=True),
    )
    all_rows, all_coef = (
        lax.all_gather(recv_rows, "dev", axis=0, tiled=True),
        lax.all_gather(recv_coef, "dev", axis=0, tiled=True),
    )
    flat_rows = all_rows.reshape(-1, model_width)
    flat_coef = all_coef.reshape(-1, EXP_GROUP)
    dev_index = lax.axis_index("dev")
    owner_expert = (dev_index * block_cols + jnp.arange(block_cols, dtype=jnp.int32)) // FF
    onehot = (owner_expert[None, :] == jnp.arange(EXP_GROUP, dtype=jnp.int32)[:, None]).astype(
        jnp.bfloat16
    )
    gate_out = jnp.dot(flat_rows, w_gate, preferred_element_type=jnp.float32)
    up_out = jnp.dot(flat_rows, w_up, preferred_element_type=jnp.float32)
    col_scale = jnp.dot(flat_coef, onehot, preferred_element_type=jnp.float32)
    hidden = (col_scale * jax.nn.silu(gate_out) * up_out).astype(jnp.bfloat16)
    partial_value = lax.optimization_barrier(
        jnp.dot(hidden, w_down, preferred_element_type=jnp.float32).astype(jnp.bfloat16)
    )
    partial_value = partial_value.reshape(dev_count, group_count, CAP, model_width)
    moved_back = lax.all_to_all(partial_value, "group", split_axis=1, concat_axis=1, tiled=True)
    summed = lax.psum_scatter(
        moved_back.astype(jnp.float32).astype(jnp.bfloat16), "dev", scatter_dimension=0, tiled=True
    )
    returned = summed.reshape(group_count, CAP, model_width)
    combined = jnp.einsum("gst,gsd->td", select_rows, returned, preferred_element_type=jnp.float32)
    return combined.astype(jnp.bfloat16)


def solution(mesh):
    return jax.shard_map(
        local,
        mesh=mesh,
        in_specs=(
            P(("group", "dev"), None),
            P(("group", "dev"), None),
            P(("group", "dev"), None),
            P(("group", "dev"), None),
            P(None, ("group", "dev")),
            P(None, ("group", "dev")),
            P(("group", "dev"), None),
        ),
        out_specs=P(("group", "dev"), None),
        check_vma=False,
    )
```

profile of v0, /device:TPU:2, one launch (start us, length us, event | category | flops | bytes accessed | tf_op | source)
XLA Modules:
  0.0 424.0 jit_solution(7251178532512982187)
XLA Ops:
  6.5 0.0 copy-start
  6.5 0.0 all-gather.2.cloned.1.call-start
  6.5 0.8 convert_reduce_fusion
  7.4 0.0 copy-done
  7.4 0.4 convolution_convert_fusion.1
  7.8 0.5 copy.26
  8.2 23.2 %all_to_all.15 = bf16[16,2,7168]{2,1,0:T(2,128)(2,1)} all-to-all(bf16[16,2,7168]{2,1,0:T(2,128)(2,1)S(1)} %copy.26), channel_id=1, replica_groups=mesh['group'=16,'dev'=16] {'group'}, dimensions={0} | all-to-all | bytes 917504 | tf_op jit(solution)/shard_map/all_to_all | solution.py:35
  31.5 0.0 all-gather.2.cloned.1.call-update
  31.5 0.1 copy.24
  31.6 0.7 convert_element_type.33
  32.3 0.8 select_reduce_fusion
  33.1 0.1 convert_element_type.35
  33.2 0.8 convolution_convert_fusion.2
  33.9 4.0 all-to-all-start
  38.0 0.0 reduce-scatter.4.cloned.1.call-start
  38.0 7.5 %all-to-all-done = bf16[16,2,4]{2,1,0:T(2,128)(2,1)S(1)} async-done(((bf16[16,2,4]{2,1,0:T(2,128)(2,1)}), bf16[16,2,4]{2,1,0:T(2,128)(2,1)S(1)}, u32[]{:S(2)}, u32[]{:S(2)}) %all-to-all-start) | async-done | bytes 288 | tf_op jit(solution)/shard_map/all_to_all | solution.py:36
  45.5 23.8 %all_gather.6 = bf16[256,2,4]{2,1,0:T(2,128)(2,1)S(1)} all-gather(bf16[16,2,4]{2,1,0:T(2,128)(2,1)S(1)} %all-to-all-done), channel_id=1, replica_groups=mesh['group'=16,'dev'=16] {'dev'}, dimensions={0}, use_global_device_ids=true | all-gather | bytes 4352 | tf_op jit(solution)/shard_map/all_gather | solution.py:40
  69.3 32.0 %all-gather.2.cloned.1.call-done = bf16[256,2,7168]{2,1,0:T(2,128)(2,1)} async-done(((bf16[16,2,7168]{2,1,0:T(2,128)(2,1)}), bf16[256,2,7168]{2,1,0:T(2,128)(2,1)}) %all-gather.2.cloned.1.call-update) | async-done | bytes 7340048 | tf_op jit(solution)/shard_map/all_gather | solution.py:39
  101.3 15.4 %reshape.40 = bf16[512,7168]{1,0:T(8,128)(2,1)} reshape(bf16[256,2,7168]{2,1,0:T(2,128)(2,1)} %all-gather.2.cloned.1.call-done) | data formatting | bytes 14680064 | tf_op jit(solution)/shard_map/reshape | solution.py:42
  116.7 0.0 copy-start.1
  116.7 0.0 copy-start.2
  116.7 6.3 %fusion.16 = f32[512,256]{1,0:T(8,128)S(1)} fusion(bf16[512,7168]{1,0:T(8,128)(2,1)} %reshape.40, bf16[7168,256]{1,0:T(8,128)(2,1)} %param.11), kind=kOutput, calls=%fused_computation.32 | convolution fusion | flops 1879048192 | bytes 11534336 | tf_op jit(solution)/shard_map/dot_general | solution.py:49
  123.1 0.0 copy-done.1
  123.1 0.9 copy-done.2
  124.0 2.1 fusion.17
  126.0 6.4 %convolution_convert_fusion = bf16[512,7168]{1,0:T(8,128)(2,1)} fusion(bf16[256,7168]{1,0:T(8,128)(2,1)} %param.13, f32[512,256]{1,0:T(8,128)S(1)} %fusion.17, bf16[512,4]{1,0:T(8,128)(2,1)S(1)} %bitcast.25, f32[512,256]{1,0:T(8,128)S(1)} %fusion.16, s32[256]{0:T(256)S(1)} %and_select_fusion), kind=kOutput, calls=%fused_computation | convolution fusion | flops 1884685312 | bytes 12063744 | tf_op jit(solution)/shard_map/dot_general | solution.py:54
  132.4 14.9 %reshape.41 = bf16[16,16,2,7168]{3,2,1,0:T(2,128)(2,1)} reshape(bf16[512,7168]{1,0:T(8,128)(2,1)} %convolution_convert_fusion) | data formatting | bytes 14680064 | tf_op jit(solution)/shard_map/reshape | solution.py:56
  147.3 6.6 %copy.27 = bf16[16,16,2,7168]{3,2,0,1:T(2,128)(2,1)S(1)} copy(bf16[16,16,2,7168]{3,2,1,0:T(2,128)(2,1)} %reshape.41) | data formatting | bytes 14680064 | tf_op jit(solution)/shard_map/reshape | solution.py:56
  153.9 168.9 %all_to_all.16 = bf16[16,16,2,7168]{3,2,0,1:T(2,128)(2,1)S(1)} all-to-all(bf16[16,16,2,7168]{3,2,0,1:T(2,128)(2,1)S(1)} %copy.27), channel_id=1, replica_groups=mesh['group'=16,'dev'=16] {'group'}, dimensions={1} | all-to-all | bytes 14680064 | tf_op jit(solution)/shard_map/all_to_all | solution.py:57
  322.8 7.0 %copy.28 = bf16[16,16,2,7168]{3,1,2,0:T(8,128)(2,1)} copy(bf16[16,16,2,7168]{3,2,0,1:T(2,128)(2,1)S(1)} %all_to_all.16) | data formatting | bytes 14680064 | tf_op jit(solution)/shard_map/all_to_all | solution.py:57
  329.8 0.0 reduce-scatter.4.cloned.1.call-update
  329.8 85.4 %reduce-scatter.4.cloned.1.call-done = bf16[1,16,2,7168]{3,1,2,0:T(8,128)(2,1)} async-done(((bf16[16,16,2,7168]{3,1,2,0:T(8,128)(2,1)}), bf16[1,16,2,7168]{3,1,2,0:T(8,128)(2,1)}) %reduce-scatter.4.cloned.1.call-update) | async-done | bytes 458768
  415.2 1.9 fusion
  (5 shorter events, 0.1 us)
Async XLA Ops:
  6.5 0.9 copy-start
  6.5 94.7 %all-gather.2.cloned.1.call-start = ((), (), s32[]{:S(2)}) async-start(), calls=%async_computation.4 | async-start | bytes 7798784 | tf_op jit(solution)/shard_map/all_gather | solution.py:39
  33.9 11.5 %all-to-all-start = ((bf16[16,2,4]{2,1,0:T(2,128)(2,1)}), bf16[16,2,4]{2,1,0:T(2,128)(2,1)S(1)}, u32[]{:S(2)}, u32[]{:S(2)}) async-start(bf16[16,2,4]{2,1,0:T(2,128)(2,1)} %convolution_convert_fusion.2), calls=%async_computation | async-start | bytes 16384 | tf_op jit(solution)/shard_map/all_to_all | solution.py:36
  38.0 377.3 %reduce-scatter.4.cloned.1.call-start = ((), (), s32[]{:S(2)}) async-start(), calls=%async_computation.5 | async-start | bytes 7798784
  116.7 6.3 %copy-start.1 = (bf16[512,7168]{1,0:T(8,128)(2,1)S(1)}, bf16[512,7168]{1,0:T(8,128)(2,1)}, u32[]{:S(2)}) copy-start(bf16[512,7168]{1,0:T(8,128)(2,1)} %reshape.40) | copy-start | bytes 22020100
  116.7 7.3 %copy-start.2 = (bf16[7168,256]{1,0:T(8,128)(2,1)S(1)}, bf16[7168,256]{1,0:T(8,128)(2,1)}, u32[]{:S(2)}) copy-start(bf16[7168,256]{1,0:T(8,128)(2,1)} %param.12) | copy-start | bytes 11010052
Sparse Core Ops, SparseCore 0:
  31.6 69.5 all-gather.1
  330.0 85.2 reduce-scatter.3
where the time goes:
time: 425 us; the launch traced here: 424 us
  blocking collectives  216 us (51%)
  waiting for transfers between devices  125 us (29%)
  local copies, waits for them, and re-layouts  45.5 us (11%)
  matrix products  17.8 us (4%)
  between operations  13.5 us (3%)
    all_to_all x1, blocking collectives, local(): lax.all_to_all(partial_value, 'group', split_axis=1, concat_axis=1, tiled...  169 us
    unnamed x3, waiting for transfers between devices  85.4 us
    all_gather x1, waiting for transfers between devices, local(): lax.all_gather(recv_rows, 'dev', axis=0, tiled=True)  32 us
    all_gather x1, blocking collectives, local(): lax.all_gather(recv_coef, 'dev', axis=0, tiled=True)  23.8 us
    all_to_all x1, blocking collectives, local(): lax.all_to_all(send_rows, 'group', split_axis=0, concat_axis=0, tiled=True)  23.2 us
    reshape x2, local copies, waits for them, and re-layouts, local(): partial_value.reshape(dev_count, group_count, CAP, model_width)  21.5 us
    reshape x1, local copies, waits for them, and re-layouts, local(): flat_rows = all_rows.reshape(-1, model_width)  15.4 us
  transfers between devices with their start and end apart: 3, of which 3 were waited for; matrix products, arithmetic and copies ran while one was open for 1% of the time, Pallas kernels for 0%

commit v1 on v0

--- a/solution.py
+++ b/solution.py
@@ -54,7 +54,10 @@
         jnp.dot(hidden, w_down, preferred_element_type=jnp.float32).astype(jnp.bfloat16)
     )
     partial_value = partial_value.reshape(dev_count, group_count, CAP, model_width)
-    moved_back = lax.all_to_all(partial_value, "group", split_axis=1, concat_axis=1, tiled=True)
+    size = lax.axis_size("group")
+    blocks = jnp.stack(jnp.split(partial_value, size, axis=1), axis=0)
+    blocks = lax.all_to_all(blocks, "group", split_axis=0, concat_axis=0)
+    moved_back = jnp.concatenate(blocks, axis=1)
     summed = lax.psum_scatter(
         moved_back.astype(jnp.float32).astype(jnp.bfloat16), "dev", scatter_dimension=0, tiled=True
     )

time: 425 us -> 430 us (1.012)
  local copies, waits for them, and re-layouts: 45.5 us -> 50.6 us
    split x0 -> x1, local copies, waits for them, and re-layouts: none -> 10.5 us  [local(): blocks = jnp.stack(jnp.split(partial_value, size, axis=1), axis=0)]
    all_to_all x1 -> x0, local copies, waits for them, and re-layouts: 6.98 us -> none  [local(): lax.all_to_all(partial_value, 'group', split_axis=1, concat_axis=1, tiled...]
    reshape x0 -> x1, local copies, waits for them, and re-layouts: none -> 6.97 us  [local(): moved_back = jnp.concatenate(blocks, axis=1)]
    reshape x2 -> x1, local copies, waits for them, and re-layouts: 21.5 us -> 14.9 us  [local(): partial_value.reshape(dev_count, group_count, CAP, model_width)]
where the time goes in v1:
time: 430 us; the launch traced here: 429 us
  blocking collectives  216 us (50%)
  waiting for transfers between devices  125 us (29%)
  local copies, waits for them, and re-layouts  50.6 us (12%)
  matrix products  17.8 us (4%)
  between operations  13.6 us (3%)
    all_to_all x1, blocking collectives, local(): blocks = lax.all_to_all(blocks, 'group', split_axis=0, concat_axis=0)  169 us
    unnamed x3, waiting for transfers between devices  85.4 us
    all_gather x1, waiting for transfers between devices, local(): lax.all_gather(recv_rows, 'dev', axis=0, tiled=True)  32 us
    all_gather x1, blocking collectives, local(): lax.all_gather(recv_coef, 'dev', axis=0, tiled=True)  23.8 us
    all_to_all x1, blocking collectives, local(): lax.all_to_all(send_rows, 'group', split_axis=0, concat_axis=0, tiled=True)  23.2 us
    reshape x1, local copies, waits for them, and re-layouts, local(): flat_rows = all_rows.reshape(-1, model_width)  15.4 us
    reshape x1, local copies, waits for them, and re-layouts, local(): partial_value.reshape(dev_count, group_count, CAP, model_width)  14.9 us
    split x1, local copies, waits for them, and re-layouts, local(): blocks = jnp.stack(jnp.split(partial_value, size, axis=1), axis=0)  10.5 us
  transfers between devices with their start and end apart: 3, of which 3 were waited for; matrix products, arithmetic and copies ran while one was open for 1% of the time, Pallas kernels for 0%

profile of v1, /device:TPU:2, one launch (start us, length us, event | category | flops | bytes accessed | tf_op | source)
XLA Modules:
  0.0 429.2 jit_solution(11863718024750651615)
XLA Ops:
  6.5 0.0 copy-start
  6.5 0.0 all-gather.2.cloned.1.call-start
  6.5 0.8 convert_reduce_fusion
  7.4 0.0 copy-done
  7.4 0.4 convolution_convert_fusion.1
  7.8 0.5 copy.107
  8.2 23.2 %all_to_all.15 = bf16[16,2,7168]{2,1,0:T(2,128)(2,1)} all-to-all(bf16[16,2,7168]{2,1,0:T(2,128)(2,1)S(1)} %copy.107), channel_id=1, replica_groups=mesh['group'=16,'dev'=16] {'group'}, dimensions={0} | all-to-all | bytes 917504 | tf_op jit(solution)/shard_map/all_to_all | solution.py:35
  31.5 0.0 all-gather.2.cloned.1.call-update
  31.5 0.1 copy.105
  31.6 0.7 convert_element_type.33
  32.3 0.8 select_reduce_fusion
  33.1 0.1 convert_element_type.35
  33.2 0.8 convolution_convert_fusion.2
  33.9 4.0 all-to-all-start
  38.0 0.0 reduce-scatter.4.cloned.1.call-start
  38.0 7.5 %all-to-all-done = bf16[16,2,4]{2,1,0:T(2,128)(2,1)S(1)} async-done(((bf16[16,2,4]{2,1,0:T(2,128)(2,1)}), bf16[16,2,4]{2,1,0:T(2,128)(2,1)S(1)}, u32[]{:S(2)}, u32[]{:S(2)}) %all-to-all-start) | async-done | bytes 288 | tf_op jit(solution)/shard_map/all_to_all | solution.py:36
  45.5 23.8 %all_gather.6 = bf16[256,2,4]{2,1,0:T(2,128)(2,1)S(1)} all-gather(bf16[16,2,4]{2,1,0:T(2,128)(2,1)S(1)} %all-to-all-done), channel_id=1, replica_groups=mesh['group'=16,'dev'=16] {'dev'}, dimensions={0}, use_global_device_ids=true | all-gather | bytes 4352 | tf_op jit(solution)/shard_map/all_gather | solution.py:40
  69.3 32.0 %all-gather.2.cloned.1.call-done = bf16[256,2,7168]{2,1,0:T(2,128)(2,1)} async-done(((bf16[16,2,7168]{2,1,0:T(2,128)(2,1)}), bf16[256,2,7168]{2,1,0:T(2,128)(2,1)}) %all-gather.2.cloned.1.call-update) | async-done | bytes 7340048 | tf_op jit(solution)/shard_map/all_gather | solution.py:39
  101.3 15.4 %reshape.46 = bf16[512,7168]{1,0:T(8,128)(2,1)} reshape(bf16[256,2,7168]{2,1,0:T(2,128)(2,1)} %all-gather.2.cloned.1.call-done) | data formatting | bytes 14680064 | tf_op jit(solution)/shard_map/reshape | solution.py:42
  116.7 0.0 copy-start.2
  116.7 0.0 copy-start.3
  116.7 6.3 %fusion.34 = f32[512,256]{1,0:T(8,128)S(1)} fusion(bf16[512,7168]{1,0:T(8,128)(2,1)} %reshape.46, bf16[7168,256]{1,0:T(8,128)(2,1)} %param.12), kind=kOutput, calls=%fused_computation.66 | convolution fusion | flops 1879048192 | bytes 11534336 | tf_op jit(solution)/shard_map/dot_general | solution.py:50
  123.0 0.0 copy-done.2
  123.1 0.9 copy-done.3
  124.0 2.1 fusion.33
  126.0 6.4 %convolution_convert_fusion = bf16[512,7168]{1,0:T(8,128)(2,1)} fusion(bf16[256,7168]{1,0:T(8,128)(2,1)} %param.13, f32[512,256]{1,0:T(8,128)S(1)} %fusion.34, bf16[512,4]{1,0:T(8,128)(2,1)S(1)} %bitcast.93, f32[512,256]{1,0:T(8,128)S(1)} %fusion.33, s32[256]{0:T(256)S(1)} %and_select_fusion), kind=kOutput, calls=%fused_computation | convolution fusion | flops 1884685312 | bytes 12063744 | tf_op jit(solution)/shard_map/dot_general | solution.py:54
  132.4 14.9 %reshape.47 = bf16[16,16,2,7168]{3,2,1,0:T(2,128)(2,1)} reshape(bf16[512,7168]{1,0:T(8,128)(2,1)} %convolution_convert_fusion) | data formatting | bytes 14680064 | tf_op jit(solution)/shard_map/reshape | solution.py:56
  147.3 10.5 %fusion.32 = (bf16[16,1,2,7168]{3,2,1,0:T(2,128)(2,1)S(1)}, bf16[16,1,2,7168]{3,2,1,0:T(2,128)(2,1)S(1)}, bf16[16,1,2,7168]{3,2,1,0:T(2,128)(2,1)S(1)}, bf16[16,...) fusion(bf16[16,16,2,7168]{3,2,1,0:T(2,128)(2,1)} %reshape.47), kind=kLoop, calls=%fused_computation.64 | loop fusion | bytes 14680064 | tf_op jit(solution)/shard_map/split | solution.py:58
  157.8 0.1 fusion.23
  157.9 0.1 fusion.22
  157.9 0.1 fusion.21
  158.0 0.1 fusion.20
  158.1 0.1 fusion.19
  158.2 0.1 fusion.18
  158.3 0.1 fusion.17
  158.4 0.1 fusion.16
  158.5 0.1 fusion.15
  158.5 0.1 fusion.14
  158.6 0.1 fusion.13
  158.7 0.1 fusion.12
  158.8 0.1 fusion.11
  158.9 0.1 fusion.10
  159.0 0.1 fusion.9
  159.1 0.1 fusion.8
  159.1 168.9 %all_to_all.16 = bf16[16,16,1,2,7168]{4,1,3,2,0:T(8,128)(2,1)S(1)} all-to-all(bf16[16,16,1,2,7168]{4,1,3,2,0:T(8,128)(2,1)S(1)} %fusion.8), channel_id=1, replica_groups=mesh['group'=16,'dev'=16] {'group'}, dimensions={0} | all-to-all | bytes 14680064 | tf_op jit(solution)/shard_map/all_to_all | solution.py:59
  328.1 0.0 copy-start.1
  328.1 7.0 %copy.124 = bf16[16,16,2,7168]{3,1,2,0:T(8,128)(2,1)} copy(bf16[16,16,2,7168]{3,0,2,1:T(8,128)(2,1)S(1)} %bitcast.92) | data formatting | bytes 14680064 | tf_op jit(solution)/shard_map/reshape | solution.py:60
  335.0 0.0 reduce-scatter.4.cloned.1.call-update
  335.1 85.4 %reduce-scatter.4.cloned.1.call-done = bf16[1,16,2,7168]{3,1,2,0:T(8,128)(2,1)} async-done(((bf16[16,16,2,7168]{3,1,2,0:T(8,128)(2,1)}), bf16[1,16,2,7168]{3,1,2,0:T(8,128)(2,1)}) %reduce-scatter.4.cloned.1.call-update) | async-done | bytes 458768
  420.5 1.9 fusion
  422.4 0.0 copy-done.1
  (5 shorter events, 0.1 us)
Async XLA Ops:
  6.5 0.9 copy-start
  6.5 94.7 %all-gather.2.cloned.1.call-start = ((), (), s32[]{:S(2)}) async-start(), calls=%async_computation.4 | async-start | bytes 7798784 | tf_op jit(solution)/shard_map/all_gather | solution.py:39
  33.9 11.5 %all-to-all-start = ((bf16[16,2,4]{2,1,0:T(2,128)(2,1)}), bf16[16,2,4]{2,1,0:T(2,128)(2,1)S(1)}, u32[]{:S(2)}, u32[]{:S(2)}) async-start(bf16[16,2,4]{2,1,0:T(2,128)(2,1)} %convolution_convert_fusion.2), calls=%async_computation | async-start | bytes 16384 | tf_op jit(solution)/shard_map/all_to_all | solution.py:36
  38.0 382.5 %reduce-scatter.4.cloned.1.call-start = ((), (), s32[]{:S(2)}) async-start(), calls=%async_computation.5 | async-start | bytes 7798784
  116.7 6.3 %copy-start.2 = (bf16[512,7168]{1,0:T(8,128)(2,1)S(1)}, bf16[512,7168]{1,0:T(8,128)(2,1)}, u32[]{:S(2)}) copy-start(bf16[512,7168]{1,0:T(8,128)(2,1)} %reshape.46) | copy-start | bytes 22020100
  116.7 7.3 %copy-start.3 = (bf16[7168,256]{1,0:T(8,128)(2,1)S(1)}, bf16[7168,256]{1,0:T(8,128)(2,1)}, u32[]{:S(2)}) copy-start(bf16[7168,256]{1,0:T(8,128)(2,1)} %param.11) | copy-start | bytes 11010052
  328.1 94.3 %copy-start.1 = (bf16[4,7168]{1,0:T(4,128)(2,1)S(1)}, bf16[4,7168]{1,0:T(4,128)(2,1)}, u32[]{:S(2)}) copy-start(bf16[4,7168]{1,0:T(4,128)(2,1)} %param.7) | copy-start | bytes 172036
Sparse Core Ops, SparseCore 0:
  31.6 69.5 all-gather.1
  335.2 85.2 reduce-scatter.3
